TPU v7x, 32 devices: a whole 2x2x4 slice. The times are simulated.
32 devices in a mesh: grp: 4 (over x, core), tok: 8 (over z, y).
Axes of the slice: x: 2, y: 2, z: 4, core: 2. Of those that a mesh axis runs over, the one named last changes fastest.
Arguments:
- layer_input: bfloat16 [32768, 768], P(('grp', 'tok')), may hold values from -6 to 6
- doc_starts: int32 [32768], P(('grp', 'tok')), may hold values 0 or 1
- ln1_gain: float32 [768], replicated, may hold values from 0.5 to 1.5
- ln1_shift: float32 [768], replicated, may hold values from -3 to 3
- w_qkv: bfloat16 [768, 2304], replicated, may hold values from -0.21875 to 0.21875
- feat_q: bfloat16 [768, 64], replicated, may hold values from -0.75 to 0.75
- feat_k: bfloat16 [768, 64], replicated, may hold values from -0.75 to 0.75
- w_out: bfloat16 [768, 768], replicated, may hold values from -6 to 6
- ln2_gain: float32 [768], replicated, may hold values from 0.5 to 1.5
- ln2_shift: float32 [768], replicated, may hold values from -3 to 3
- w_fc: bfloat16 [768, 3072], replicated, may hold values from -0.21875 to 0.21875
- w_proj: bfloat16 [3072, 768], replicated, may hold values from -0.109375 to 0.109375
- cotangent: bfloat16 [32768, 768], P(('grp', 'tok')), may hold values from -6 to 6
Outputs:
- output: bfloat16 [32768, 768], P(('grp', 'tok'))
- grad_input: float32 [32768, 768], P(('grp', 'tok'))
- grad_ln1_gain: float32 [768], P('tok')
- grad_ln1_shift: float32 [768], P('tok')
- grad_qkv: float32 [768, 2304], P('tok')
- grad_feat_q: float32 [768, 64], P('tok')
- grad_feat_k: float32 [768, 64], P('tok')
- grad_w_out: float32 [768, 768], P('tok')
- grad_ln2_gain: float32 [768], P('tok')
- grad_ln2_shift: float32 [768], P('tok')
- grad_fc: float32 [768, 3072], P('tok')
- grad_proj: float32 [3072, 768], P('tok')
Inputs may be any that keep to these rules, and one draw needn't show every extreme that they name: `doc_starts`: 1 marks the first token of a document; attention and carried sums stop there.
All inputs are finite; a program needn't handle non-finite values. No bound on the sum of `doc_starts` on one device may be relied on, other than what follows from the above.
Results may differ from a plain program's by a relative error of at most 0.011.
Values sent between devices are 32-bit elements; how exact they have to be, the bound alone decides.
No kernel may reach another device: no remote copies, remote signals or barrier semaphores. Data moves between devices by JAX's collectives and lax.ppermute only.
A program may use at most 768 MiB of HBM per device.

v0:
```python
from functools import partial

import jax
import jax.numpy as jnp
from jax import lax
from jax.sharding import PartitionSpec as P

eps = 1e-05
highest = lax.Precision.HIGHEST


def entering(value, axis, join, neutral, backward):
    count, mine = (lax.axis_size(axis), lax.axis_index(axis))
    pieces = jax.tree.map(lambda part: lax.all_gather(part, axis), value)
    if backward:
        pieces = jax.tree.map(lambda part: part[::-1], pieces)
        mine = count - 1 - mine
    so_far = jax.tree.map(
        lambda part, zero: jnp.full_like(part, 0) + jnp.asarray(zero, part.dtype), value, neutral
    )

    def hop(position, so_far):
        longer = join(so_far, jax.tree.map(lambda part: part[position], pieces))
        return jax.tree.map(lambda new, old: jnp.where(position < mine, new, old), longer, so_far)

    return lax.fori_loop(0, count - 1, hop, so_far)


def layer_norm(value, gain, shift):
    centre = jnp.mean(value, axis=-1, keepdims=True)
    centered = value - centre
    variance = jnp.mean(centered * centered, axis=-1, keepdims=True)
    return centered * lax.rsqrt(variance + eps) * gain + shift


def feature_map(logits):
    return jnp.concatenate(
        [jax.nn.softmax(logits, axis=-1), jax.nn.softmax(-logits, axis=-1)], axis=-1
    )


def chain_step(earlier, later):
    flag_early, state_early, normer_early = earlier
    flag_late, state_late, normer_late = later
    retain = 1.0 - flag_late
    return (
        jnp.maximum(flag_early, flag_late),
        state_late + retain * state_early,
        normer_late + retain * normer_early,
    )


def on_device(
    layer_input,
    doc_starts,
    ln1_gain,
    ln1_shift,
    w_qkv,
    feat_q,
    feat_k,
    w_out,
    ln2_gain,
    ln2_shift,
    w_fc,
    w_proj,
    cotangent,
):
    tokens, model_width = layer_input.shape
    head_dim = feat_q.shape[1]
    head_count = model_width // head_dim
    block_rows = min(512, tokens)
    xfloat = layer_input.astype(jnp.float32)
    normed1, ln1_back = jax.vjp(layer_norm, xfloat, ln1_gain, ln1_shift)
    hidden1 = normed1.astype(jnp.bfloat16)
    packed = jnp.dot(hidden1, w_qkv, preferred_element_type=jnp.float32).astype(jnp.bfloat16)
    queries = packed[:, :model_width].reshape(tokens, head_count, head_dim)
    key_vals = packed[:, model_width : 2 * model_width].reshape(tokens, head_count, head_dim)
    values = packed[:, 2 * model_width :].reshape(tokens, head_count, head_dim)
    maps_query = feat_q.reshape(head_count, head_dim, head_dim)
    maps_key = feat_k.reshape(head_count, head_dim, head_dim)
    logit_query = jnp.einsum(
        "thi,hij->thj", queries, maps_query, preferred_element_type=jnp.float32
    )
    logit_key = jnp.einsum("thi,hij->thj", key_vals, maps_key, preferred_element_type=jnp.float32)
    feat_query, query_back = jax.vjp(feature_map, logit_query)
    feat_key, key_back = jax.vjp(feature_map, logit_key)
    phi_query = feat_query.astype(jnp.bfloat16)
    phi_key = feat_key.astype(jnp.bfloat16)
    segment = jnp.cumsum(doc_starts)
    position = jnp.arange(tokens)
    opened = (segment == 0).astype(jnp.float32)
    closing = segment == segment[-1]
    reset_flag = jnp.minimum(segment[-1], 1).astype(jnp.float32)
    tail_keys = jnp.where(closing[:, None, None], phi_key, jnp.zeros_like(phi_key))
    state_local = jnp.einsum("shf,shd->hfd", tail_keys, values, preferred_element_type=jnp.float32)
    normer_local = jnp.sum(tail_keys, axis=0, dtype=jnp.float32)
    carried = entering(
        (reset_flag, state_local, normer_local),
        ("grp", "tok"),
        chain_step,
        (jnp.zeros((), jnp.float32), jnp.zeros_like(state_local), jnp.zeros_like(normer_local)),
        False,
    )
    state_in = carried[1]
    normer_in = carried[2]

    def block_weights(offset):
        scores = jnp.einsum(
            "thf,shf->hts",
            phi_query[offset : offset + block_rows],
            phi_key,
            preferred_element_type=jnp.float32,
        )
        allowed = (position[offset : offset + block_rows, None] >= position[None, :]) & (
            segment[offset : offset + block_rows, None] == segment[None, :]
        )
        return (allowed, jnp.where(allowed[None], scores, 0.0).astype(jnp.bfloat16))

    mixed_parts = []
    denom_parts = []
    for offset in range(0, tokens, block_rows):
        allowed, weights = block_weights(offset)
        open_rows = opened[offset : offset + block_rows]
        query_wide = phi_query[offset : offset + block_rows].astype(jnp.float32)
        numer_local = jnp.einsum(
            "hts,shd->thd", weights, values, preferred_element_type=jnp.float32
        )
        numer_carry = open_rows[:, None, None] * jnp.einsum(
            "thf,hfd->thd", query_wide, state_in, precision=highest
        )
        denominator = jnp.sum(weights, axis=2, dtype=jnp.float32).T + open_rows[
            :, None
        ] * jnp.einsum("thf,hf->th", query_wide, normer_in, precision=highest)
        mixed_parts.append((numer_local + numer_carry) / denominator[:, :, None])
        denom_parts.append(denominator)
    mixed_all = jnp.concatenate(mixed_parts, axis=0)
    denom_all = jnp.concatenate(denom_parts, axis=0)
    mixed_low = mixed_all.reshape(tokens, model_width).astype(jnp.bfloat16)
    resid = xfloat + jnp.dot(mixed_low, w_out, preferred_element_type=jnp.float32)
    normed2, ln2_back = jax.vjp(layer_norm, resid, ln2_gain, ln2_shift)
    hidden2 = normed2.astype(jnp.bfloat16)
    pre_act = jnp.dot(hidden2, w_fc, preferred_element_type=jnp.float32)
    activ, gelu_back = jax.vjp(partial(jax.nn.gelu, approximate=True), pre_act)
    act_low = activ.astype(jnp.bfloat16)
    output = (resid + jnp.dot(act_low, w_proj, preferred_element_type=jnp.float32)).astype(
        jnp.bfloat16
    )
    grad_proj = jnp.dot(act_low.T, cotangent, preferred_element_type=jnp.float32)
    dact = jnp.dot(cotangent, w_proj.T, preferred_element_type=jnp.float32)
    dpre = gelu_back(dact)[0].astype(jnp.bfloat16)
    grad_fc = jnp.dot(hidden2.T, dpre, preferred_element_type=jnp.float32)
    dhidden2 = jnp.dot(dpre, w_fc.T, preferred_element_type=jnp.float32)
    dresid_norm, grad_g2, grad_b2 = ln2_back(dhidden2)
    dresid = cotangent.astype(jnp.float32) + dresid_norm
    dbranch = dresid.astype(jnp.bfloat16)
    grad_out = jnp.dot(mixed_low.T, dbranch, preferred_element_type=jnp.float32)
    dmixed = jnp.dot(dbranch, w_out.T, preferred_element_type=jnp.float32).reshape(
        tokens, head_count, head_dim
    )
    grad_phiq_parts = []
    grad_phik = jnp.zeros((tokens, head_count, 2 * head_dim), jnp.float32)
    grad_values = jnp.zeros((tokens, head_count, head_dim), jnp.float32)
    grad_state = jnp.zeros_like(state_local)
    grad_normer = jnp.zeros_like(normer_local)
    for offset in range(0, tokens, block_rows):
        allowed, weights = block_weights(offset)
        open_rows = opened[offset : offset + block_rows]
        query_rows = phi_query[offset : offset + block_rows]
        query_wide = query_rows.astype(jnp.float32)
        denominator = denom_all[offset : offset + block_rows]
        dmixed_rows = dmixed[offset : offset + block_rows]
        dnumer = dmixed_rows / denominator[:, :, None]
        ddenom = (
            -jnp.sum(dmixed_rows * mixed_all[offset : offset + block_rows], axis=2) / denominator
        )
        dnumer_low = dnumer.astype(jnp.bfloat16)
        dweights = (
            jnp.einsum("thd,shd->hts", dnumer_low, values, preferred_element_type=jnp.float32)
            + ddenom.T[:, :, None]
        )
        dweights = jnp.where(allowed[None], dweights, 0.0).astype(jnp.bfloat16)
        grad_query = jnp.einsum(
            "hts,shf->thf", dweights, phi_key, preferred_element_type=jnp.float32
        )
        grad_query = grad_query + open_rows[:, None, None] * (
            jnp.einsum("thd,hfd->thf", dnumer, state_in, precision=highest)
            + ddenom[:, :, None] * normer_in[None]
        )
        grad_phiq_parts.append(grad_query)
        grad_phik = grad_phik + jnp.einsum(
            "hts,thf->shf", dweights, query_rows, preferred_element_type=jnp.float32
        )
        grad_values = grad_values + jnp.einsum(
            "hts,thd->shd", weights, dnumer_low, preferred_element_type=jnp.float32
        )
        open_query = query_wide * open_rows[:, None, None]
        grad_state = grad_state + jnp.einsum("thf,thd->hfd", open_query, dnumer, precision=highest)
        grad_normer = grad_normer + jnp.einsum("th,thf->hf", ddenom, open_query, precision=highest)
    returned = entering(
        (reset_flag, grad_state, grad_normer),
        ("grp", "tok"),
        chain_step,
        (jnp.zeros((), jnp.float32), jnp.zeros_like(grad_state), jnp.zeros_like(grad_normer)),
        True,
    )
    back_state = returned[1]
    back_normer = returned[2]
    closing_wide = closing.astype(jnp.float32)[:, None, None]
    grad_phik = grad_phik + closing_wide * (
        jnp.einsum("shd,hfd->shf", values.astype(jnp.float32), back_state, precision=highest)
        + back_normer[None]
    )
    grad_values = grad_values + closing_wide * jnp.einsum(
        "shf,hfd->shd", phi_key.astype(jnp.float32), back_state, precision=highest
    )
    grad_phiq = jnp.concatenate(grad_phiq_parts, axis=0)
    dlogit_query = query_back(grad_phiq)[0].astype(jnp.bfloat16)
    dlogit_key = key_back(grad_phik)[0].astype(jnp.bfloat16)
    grad_featq = jnp.einsum(
        "thi,thj->hij", queries, dlogit_query, preferred_element_type=jnp.float32
    ).reshape(model_width, head_dim)
    grad_featk = jnp.einsum(
        "thi,thj->hij", key_vals, dlogit_key, preferred_element_type=jnp.float32
    ).reshape(model_width, head_dim)
    dqueries = jnp.einsum(
        "thj,hij->thi", dlogit_query, maps_query, preferred_element_type=jnp.float32
    )
    dkeys = jnp.einsum("thj,hij->thi", dlogit_key, maps_key, preferred_element_type=jnp.float32)
    dpacked = jnp.concatenate(
        [
            dqueries.reshape(tokens, model_width),
            dkeys.reshape(tokens, model_width),
            grad_values.reshape(tokens, model_width),
        ],
        axis=1,
    ).astype(jnp.bfloat16)
    grad_qkv = jnp.dot(hidden1.T, dpacked, preferred_element_type=jnp.float32)
    dhidden1 = jnp.dot(dpacked, w_qkv.T, preferred_element_type=jnp.float32)
    dx_norm, grad_g1, grad_b1 = ln1_back(dhidden1)
    grad_input = dresid + dx_norm
    norm_stack = jnp.stack([grad_g1, grad_b1, grad_g2, grad_b2], axis=1)
    shares = (
        lax.psum_scatter(norm_stack, "tok", scatter_dimension=0, tiled=True),
        lax.psum_scatter(grad_qkv, "tok", scatter_dimension=0, tiled=True),
        lax.psum_scatter(grad_featq, "tok", scatter_dimension=0, tiled=True),
        lax.psum_scatter(grad_featk, "tok", scatter_dimension=0, tiled=True),
        lax.psum_scatter(grad_out, "tok", scatter_dimension=0, tiled=True),
        lax.psum_scatter(grad_fc, "tok", scatter_dimension=0, tiled=True),
        lax.psum_scatter(grad_proj, "tok", scatter_dimension=0, tiled=True),
    )
    shares = lax.psum(
        (shares[0], shares[1], shares[2], shares[3], shares[4], shares[5], shares[6]), "grp"
    )
    return (
        output,
        grad_input,
        shares[0][:, 0],
        shares[0][:, 1],
        shares[1],
        shares[2],
        shares[3],
        shares[4],
        shares[0][:, 2],
        shares[0][:, 3],
        shares[5],
        shares[6],
    )


def solution(mesh):
    in_specs = (
        P(("grp", "tok"), None),
        P(("grp", "tok")),
        P(),
        P(),
        P(),
        P(),
        P(),
        P(),
        P(),
        P(),
        P(),
        P(),
        P(("grp", "tok"), None),
    )
    out_specs = (
        P(("grp", "tok"), None),
        P(("grp", "tok"), None),
        P("tok"),
        P("tok"),
        P("tok", None),
        P("tok", None),
        P("tok", None),
        P("tok", None),
        P("tok"),
        P("tok"),
        P("tok", None),
        P("tok", None),
    )
    return jax.shard_map(
        on_device, mesh=mesh, in_specs=in_specs, out_specs=out_specs, check_vma=False
    )
```

profile of v0, /device:TPU:0, one launch (start us, length us, event | category | flops | bytes accessed | tf_op | source)
XLA Modules:
  0.0 1471.4 jit_solution(9644672946341069349)
XLA Ops:
  49.3 43.0 %all-reduce = f32[32]{0:T(128)} all-reduce(f32[32]{0:T(128)S(1)} %dynamic-update-slice), channel_id=1, replica_groups=mesh['grp'=4,'tok'=8] {'grp','tok'}, use_global_device_ids=true, to_apply=%add | all-reduce | flops 32 | bytes 256
  102.9 75.4 %all-gather.4 = f32[32,12,128]{2,1,0:T(8,128)} all-gather(f32[1,12,128]{2,1,0:T(8,128)S(1)} %bitcast.295), channel_id=3, replica_groups=mesh['grp'=4,'tok'=8] {'grp','tok'}, dimensions={0}, use_global_device_ids=true | all-gather | bytes 202752 | tf_op jit(solution)/shard_map/all_gather | solution.py:14
  195.1 7.9 convert_reduce_fusion
  203.0 9.7 fusion.111
  212.7 7.9 convert_reduce_fusion.1
  220.6 9.7 fusion.110
  230.3 254.4 %while.32 = (s32[]{:T(128)}, f32[12,128,64]{2,1,0:T(8,128)}, f32[12,128]{1,0:T(8,128)S(1)}, s32[]{:T(128)}, f32[32,12,128,64]{2,3,1,0:T(8,128)}, /*index=5*/f32[...) while((s32[]{:T(128)}, f32[12,128,64]{2,1,0:T(8,128)}, ...), condition=%wide.region_14.15_spmd.clone, body=%wide.region_13.14_spmd.clone.sunk | while | flops 399365 | bytes 2771115 | solution.py:26
  506.8 16.8 %fusion.14 = bf16[1024,3072]{1,0:T(8,128)(2,1)} fusion(f32[1024,3072]{1,0:T(8,128)S(1)} %fusion.92, bf16[1024,768]{1,0:T(8,128)(2,1)S(1)} %copy-done.49, bf16[3072,768]{1,0:T(8,128)(2,1)} %param.28), kind=kOutput, calls=%fused_computation.27 | convolution fusion | flops 4894752768 | bytes 25165824 | tf_op jit(solution)/shard_map/dot_general | solution.py:149
  523.6 10.4 fusion.108
  562.0 13.1 fusion.95
  587.9 72.5 %all-gather.5 = f32[32,12,128]{2,1,0:T(8,128)} all-gather(f32[1,12,128]{2,1,0:T(8,128)S(1)} %fusion.79), channel_id=5, replica_groups=mesh['grp'=4,'tok'=8] {'grp','tok'}, dimensions={0}, use_global_device_ids=true | all-gather | bytes 202752 | tf_op jit(solution)/shard_map/all_gather | solution.py:14
  664.3 9.2 select_convert_fusion.1
  673.5 11.8 fusion.94
  685.3 7.4 fusion.30
  692.7 7.7 select_convert_fusion
  700.4 11.7 fusion.93
  731.4 10.4 fusion.113
  751.5 10.6 fusion.91
  762.2 18.0 %copy.128 = f32[32,12,128,64]{3,2,1,0:T(8,128)} copy(f32[32,12,128,64]{2,3,1,0:T(8,128)} %bitcast.269) | data formatting | bytes 25165824 | tf_op jit(solution)/shard_map/all_gather | solution.py:14
  780.3 17.5 %rev.9 = f32[32,12,128,64]{3,2,1,0:T(8,128)} reverse(f32[32,12,128,64]{3,2,1,0:T(8,128)} %copy.128), dimensions={0} | reverse | bytes 25165824 | tf_op jit(solution)/shard_map/rev | solution.py:16
  797.8 133.7 %while.33 = (s32[]{:T(128)}, f32[12,128,64]{2,1,0:T(8,128)}, f32[12,128]{1,0:T(8,128)S(1)}, s32[]{:T(128)}, f32[32,12,128,64]{3,2,1,0:T(8,128)}, /*index=5*/f32[...) while((s32[]{:T(128)}, f32[12,128,64]{2,1,0:T(8,128)}, ...), condition=%wide.region_26.27_spmd.clone, body=%wide.region_25.26_spmd.clone.sunk | while | flops 399365 | bytes 1198251 | solution.py:26
  931.5 9.1 add_bitcast_fusion
  952.7 6.9 fusion.49
  964.9 7.9 fusion.109
  987.3 66.7 %reduce-scatter.18.cloned.1.call-done = f32[96,3072]{1,0:T(8,128)} async-done(((f32[768,3072]{1,0:T(8,128)}), f32[96,3072]{1,0:T(8,128)}) %reduce-scatter.18.cloned.1.call-update) | async-done | bytes 1179664 | tf_op jit(solution)/shard_map/reduce_scatter | solution.py:248
  1053.9 131.8 %reduce-scatter.14.cloned.1.call-done = f32[96,2304]{1,0:T(8,128)} async-done(((f32[768,2304]{1,0:T(8,128)}), f32[96,2304]{1,0:T(8,128)}) %reduce-scatter.14.cloned.1.call-update) | async-done | bytes 884752 | tf_op jit(solution)/shard_map/reduce_scatter | solution.py:244
  1185.7 12.0 add_convert_fusion.3
  1200.3 50.6 %reduce-scatter.24.cloned.1.call-done = f32[96,64]{1,0:T(8,128)} async-done(((f32[768,64]{1,0:T(8,128)}), f32[96,64]{1,0:T(8,128)}) %reduce-scatter.24.cloned.1.call-update) | async-done | bytes 24592
  1263.5 52.5 %reduce-scatter.22.cloned.1.call-done = f32[96,4]{1,0:T(8,128)} async-done(((f32[768,4]{1,0:T(8,128)}), f32[96,4]{1,0:T(8,128)}) %reduce-scatter.22.cloned.1.call-update) | async-done | bytes 1552
  1316.9 64.2 %reduce-scatter.26.cloned.1.call-done = f32[96,64]{1,0:T(8,128)} async-done(((f32[768,64]{1,0:T(8,128)}), f32[96,64]{1,0:T(8,128)}) %reduce-scatter.26.cloned.1.call-update) | async-done | bytes 24592
  1382.6 13.4 all-reduce.1
  1396.5 61.5 %all-reduce.5.cloned.1.call-done = (f32[96,2304]{1,0:T(8,128)}, f32[96,768]{1,0:T(8,128)}, f32[96,3072]{1,0:T(8,128)}, f32[384,768]{1,0:T(8,128)}) async-done(((f32[96,2304]{1,0:T(8,128)}, f32[96,768]{1,0:T(8,128)}, f32[96,3072]{1,0:T(8,128)}, f32[384,768]{1,0:T(8,128)}), (f32[96,2304]{1,0:T(8,128)}, f32[96,768]{1,0:T(8,128)}, f32[96,3072]{1,0:T(8,128)}, f32[384,768]{1,0:T(8,128)})) %all-reduce.5.cloned.1.call-update) | async-done | bytes 3538960 | tf_op jit(solution)/shard_map/psum | solution.py:251
  (675 shorter events, 566.4 us)
Async XLA Ops:
  7.2 223.1 %all-gather.9.cloned.1.call-start = ((), (), s32[]{:S(2)}) async-start(), calls=%async_computation.11 | async-start | bytes 12976128 | tf_op jit(solution)/shard_map/all_gather | solution.py:14
  48.5 713.8 %all-gather.11.cloned.1.call-start = ((), (), s32[]{:S(2)}) async-start(), calls=%async_computation.12 | async-start | bytes 12976128 | tf_op jit(solution)/shard_map/all_gather | solution.py:14
  192.5 10.5 copy-start.32
  192.5 20.2 %copy-start.37 = (bf16[512,12,128]{0,2,1:T(8,128)(2,1)}, bf16[512,12,128]{0,2,1:T(8,128)(2,1)S(1)}, u32[]{:S(2)}) copy-start(bf16[512,12,128]{0,2,1:T(8,128)(2,1)S(1)} %get-tuple-element.425) | copy-start | bytes 4718596
  193.3 295.9 %copy-start.110 = (f32[512]{0:T(512)}, f32[512]{0:T(512)S(1)}, u32[]{:S(2)}) copy-start(f32[512]{0:T(512)S(1)} %get-tuple-element.428) | copy-start | bytes 6148
  194.4 18.3 %copy-start.74 = (pred[512,1024]{1,0:T(8,128)(4,1)}, pred[512,1024]{1,0:T(8,128)(4,1)S(1)}, u32[]{:S(2)}) copy-start(pred[512,1024]{1,0:T(8,128)(4,1)S(1)} %get-tuple-element.429) | copy-start | bytes 1572868
  220.6 9.7 copy-start.128
  506.8 16.9 %copy-start.46 = (f32[1024,3072]{1,0:T(8,128)}, f32[1024,3072]{1,0:T(8,128)S(1)}, u32[]{:S(2)}) copy-start(f32[1024,3072]{1,0:T(8,128)S(1)} %fusion.92) | copy-start | bytes 37748740
  557.1 430.1 %reduce-scatter.16.cloned.1.call-start = ((), (), s32[]{:S(2)}) async-start(), calls=%async_computation.8 | async-start | bytes 2654208 | tf_op jit(solution)/shard_map/reduce_scatter | solution.py:247
  561.9 425.4 %reduce-scatter.20.cloned.1.call-start = ((), (), s32[]{:S(2)}) async-start(), calls=%async_computation.10 | async-start | bytes 10616832 | tf_op jit(solution)/shard_map/reduce_scatter | solution.py:249
  575.1 478.9 %reduce-scatter.18.cloned.1.call-start = ((), (), s32[]{:S(2)}) async-start(), calls=%async_computation.9 | async-start | bytes 10616832 | tf_op jit(solution)/shard_map/reduce_scatter | solution.py:248
  726.4 15.4 %slice-start = ((s8[12582912]{0:T(1024)(128)(4,1)}), s8[4194304]{0:T(1024)(128)(4,1)S(1)}, s32[]{:S(2)}) async-start(s8[12582912]{0:T(1024)(128)(4,1)} %bitcast.241), calls=%async_computation.17 | async-start | bytes 8388608
  726.4 15.4 %slice-start.1 = ((s8[12582912]{0:T(1024)(128)(4,1)}), s8[4194304]{0:T(1024)(128)(4,1)S(1)}, s32[]{:S(2)}) async-start(s8[12582912]{0:T(1024)(128)(4,1)} %bitcast.241), calls=%async_computation.18 | async-start | bytes 8388608
  731.4 10.4 slice-start.2
  731.4 10.4 copy-start.67
  731.4 16.1 %slice-start.3 = ((s8[12582912]{0:T(1024)(128)(4,1)}), s8[4194304]{0:T(1024)(128)(4,1)S(1)}, s32[]{:S(2)}) async-start(s8[12582912]{0:T(1024)(128)(4,1)} %bitcast.243), calls=%async_computation.20 | async-start | bytes 8388608
  731.4 16.1 %slice-start.4 = ((s8[12582912]{0:T(1024)(128)(4,1)}), s8[4194304]{0:T(1024)(128)(4,1)S(1)}, s32[]{:S(2)}) async-start(s8[12582912]{0:T(1024)(128)(4,1)} %bitcast.243), calls=%async_computation.21 | async-start | bytes 8388608
  762.2 423.6 %reduce-scatter.14.cloned.1.call-start = ((), (), s32[]{:S(2)}) async-start(), calls=%async_computation.7 | async-start | bytes 7962624 | tf_op jit(solution)/shard_map/reduce_scatter | solution.py:244
  780.3 17.5 %copy-start.80 = (f32[12,128]{1,0:T(8,128)S(1)}, f32[12,128]{1,0:T(8,128)}, u32[]{:S(2)}) copy-start(f32[12,128]{1,0:T(8,128)} %custom-call.3) | copy-start | bytes 18436
  780.3 17.5 %copy-start.129 = (f32[32]{0:T(128)S(1)}, f32[32]{0:T(128)}, u32[]{:S(2)}) copy-start(f32[32]{0:T(128)} %rev.10) | copy-start | bytes 388
  797.8 133.7 %copy-start.108 = (f32[1024]{0:T(1024)S(1)}, f32[1024]{0:T(1024)}, u32[]{:S(2)}) copy-start(f32[1024]{0:T(1024)} %get-tuple-element.414) | copy-start | bytes 12292
  931.5 9.1 copy-start.5
  931.5 9.2 copy-start.6
  931.5 9.2 copy-start.83
  931.5 9.2 copy-start.84
  959.6 291.3 %reduce-scatter.24.cloned.1.call-start = ((), (), s32[]{:S(2)}) async-start(), calls=%async_computation.14 | async-start | bytes 442368
  964.8 351.2 %reduce-scatter.22.cloned.1.call-start = ((), (), s32[]{:S(2)}) async-start(), calls=%async_computation.13 | async-start | bytes 442368
  983.8 397.3 %reduce-scatter.26.cloned.1.call-start = ((), (), s32[]{:S(2)}) async-start(), calls=%async_computation.15 | async-start | bytes 442368
  987.2 470.8 %all-reduce.5.cloned.1.call-start = ((), (), s32[]{:S(2)}) async-start(), calls=%async_computation.16 | async-start | bytes 7077888 | tf_op jit(solution)/shard_map/psum | solution.py:251
  1197.7 55.4 %copy-start.96 = (f32[1024]{0:T(1024)S(1)}, f32[1024]{0:T(1024)}, u32[]{:S(2)}) copy-start(f32[1024]{0:T(1024)} %copy-done.95) | copy-start | bytes 12292
  1197.7 55.4 %copy-start.99 = (f32[1024]{0:T(1024)S(1)}, f32[1024]{0:T(1024)}, u32[]{:S(2)}) copy-start(f32[1024]{0:T(1024)} %copy-done.97) | copy-start | bytes 12292
  1197.7 55.4 %copy-start.106 = (f32[768]{0:T(1024)S(1)}, f32[768]{0:T(1024)}, u32[]{:S(2)}) copy-start(f32[768]{0:T(1024)} %param.19) | copy-start | bytes 9220
  (119 other events, 485.0 us)
Sparse Core Ops, SparseCore 0:
  48.6 101.3 all-gather.8
  557.3 94.0 all-gather.10
  654.9 68.4 reduce-scatter.15
  726.8 161.3 reduce-scatter.19
  891.6 162.2 reduce-scatter.17
  1057.5 128.2 reduce-scatter.13
  1189.6 61.3 reduce-scatter.23
  1254.8 61.1 reduce-scatter.21
  1319.9 61.2 reduce-scatter.25
  1383.6 74.3 all-reduce.4
where the time goes:
time: 1490 us; the launch traced here: 1470 us
  waiting for transfers between devices  428 us (29%)
  matrix products  277 us (19%)
  local copies, waits for them, and re-layouts  260 us (17%)
  other arithmetic  244 us (16%)
  blocking collectives  204 us (14%)
  loops' own time  40.7 us (3%)
  between operations  17 us (1%)
    select_n x124, other arithmetic, hop(): jnp.where(position < mine, new, old)  190 us
    unnamed x13, waiting for transfers between devices  168 us
    dynamic_slice x124, local copies, waits for them, and re-layouts, hop(): longer = join(so_far, jax.tree.map(lambda part: part[position], pieces))  157 us
    all_gather x2, blocking collectives, entering(): pieces = jax.tree.map(lambda part: lax.all_gather(part, axis), value)  148 us
    reduce_scatter x1, waiting for transfers between devices, on_device(): lax.psum_scatter(grad_qkv, 'tok', scatter_dimension=0, tiled=True)  132 us
    reduce_scatter x1, waiting for transfers between devices, on_device(): lax.psum_scatter(grad_fc, 'tok', scatter_dimension=0, tiled=True)  66.7 us
    psum x1, waiting for transfers between devices, on_device(): lax.psum((shares[0], shares[1], shares[2], shares[3], shares[4], shares[5...  61.5 us
    unnamed x1, blocking collectives  43 us
  transfers between devices with their start and end apart: 10, of which 6 were waited for; matrix products, arithmetic and copies ran while one was open for 29% of the time, Pallas kernels for 0%

commit v1 on v0

--- a/solution.py
+++ b/solution.py
@@ -9,21 +9,93 @@
 highest = lax.Precision.HIGHEST
 
 
-def entering(value, axis, join, neutral, backward):
-    count, mine = (lax.axis_size(axis), lax.axis_index(axis))
-    pieces = jax.tree.map(lambda part: lax.all_gather(part, axis), value)
-    if backward:
-        pieces = jax.tree.map(lambda part: part[::-1], pieces)
-        mine = count - 1 - mine
-    so_far = jax.tree.map(
-        lambda part, zero: jnp.full_like(part, 0) + jnp.asarray(zero, part.dtype), value, neutral
-    )
-
-    def hop(position, so_far):
-        longer = join(so_far, jax.tree.map(lambda part: part[position], pieces))
-        return jax.tree.map(lambda new, old: jnp.where(position < mine, new, old), longer, so_far)
-
-    return lax.fori_loop(0, count - 1, hop, so_far)
+def log2_of(count):
+    return count.bit_length() - 1
+
+
+def flips(grp_size, tok_size, first, second):
+    pairs = []
+    for place in range(grp_size * tok_size):
+        grp = place // tok_size
+        pairs.append((place, place ^ (second if grp % 2 else first)))
+    return pairs
+
+
+def carry_scan(packed, keep, backward):
+    grp_size, tok_size = (lax.axis_size("grp"), lax.axis_size("tok"))
+    place = lax.axis_index("grp") * tok_size + lax.axis_index("tok")
+    rows = packed.shape[0]
+    total = jnp.concatenate([packed, jnp.full((4, 128), keep, jnp.float32)], axis=0)
+    is_keep = lax.broadcasted_iota(jnp.int32, total.shape, 0) >= rows
+    prefix = jnp.where(is_keep, 1.0, 0.0)
+    steps = log2_of(grp_size * tok_size)
+    for step in range(steps):
+        other = lax.ppermute(total, ("grp", "tok"), flips(grp_size, tok_size, 1 << step, 1 << step))
+        bit = (place >> step) & 1
+        later = (bit == 0) if backward else (bit == 1)
+        prefix = jnp.where(later, jnp.where(is_keep, 0.0, prefix) + prefix[rows, 0] * other, prefix)
+        if step + 1 < steps:
+            late = jnp.where(later, total, other)
+            early = jnp.where(later, other, total)
+            total = jnp.where(is_keep, 0.0, late) + late[rows, 0] * early
+    return prefix[:rows]
+
+
+def reduce_rows(grad):
+    grp_size, tok_size = (lax.axis_size("grp"), lax.axis_size("tok"))
+    axes = ("grp", "tok")
+    core = lax.axis_index("grp") % 2
+    place = lax.axis_index("grp") * tok_size + lax.axis_index("tok")
+    tok_bits, far_bits = (log2_of(tok_size), log2_of(grp_size) - 1)
+    width = grad.shape[1]
+    rows = grad.shape[0] // tok_size
+    sub = rows // grp_size
+    far = grp_size // 2
+    view = grad.reshape(tok_size, 2, far * sub, width)
+    mine = lax.dynamic_index_in_dim(view, core, 1, keepdims=False)
+    theirs = lax.dynamic_index_in_dim(view, 1 - core, 1, keepdims=False)
+    mine = mine + lax.ppermute(theirs, axes, flips(grp_size, tok_size, tok_size, tok_size))
+    dims = (2,) * (tok_bits + far_bits)
+    mine = mine.reshape(dims + (sub, width))
+    tok_axes = list(range(tok_bits))[::-1]
+    far_axes = [tok_bits + i for i in range(far_bits)][::-1]
+    order_a = far_axes + tok_axes
+    order_b = tok_axes + far_axes
+    tail = (len(dims), len(dims) + 1)
+    buf = jnp.where(
+        core == 0,
+        mine.transpose(*order_a, *tail),
+        mine.transpose(*order_b, *tail),
+    ).reshape(-1, sub, width)
+    tok_flips = [1 << i for i in range(tok_bits)]
+    far_flips = [(2 * tok_size) << i for i in range(far_bits)]
+    flips_a = far_flips + tok_flips
+    flips_b = tok_flips + far_flips
+    for flip_a, flip_b in zip(flips_a, flips_b):
+        bit = jnp.where(core == 0, (place & flip_a) != 0, (place & flip_b) != 0).astype(jnp.int32)
+        half = buf.shape[0] // 2
+        keep = lax.dynamic_slice_in_dim(buf, bit * half, half, 0)
+        give = lax.dynamic_slice_in_dim(buf, (1 - bit) * half, half, 0)
+        buf = keep + lax.ppermute(give, axes, flips(grp_size, tok_size, flip_a, flip_b))
+    for flip in far_flips + [tok_size]:
+        bit = (place & flip) != 0
+        other = lax.ppermute(buf, axes, flips(grp_size, tok_size, flip, flip))
+        buf = jnp.concatenate(
+            [jnp.where(bit, other, buf), jnp.where(bit, buf, other)], axis=0
+        )
+    return buf.reshape(rows, width)
+
+
+def reduce_vectors(stack):
+    grp_size, tok_size = (lax.axis_size("grp"), lax.axis_size("tok"))
+    count, length = stack.shape
+    share = length // tok_size
+    blocks = stack.reshape(count, tok_size, share).transpose(1, 0, 2)
+    blocks = blocks.reshape(tok_size, count * share)
+    spread = jnp.broadcast_to(blocks[None], (grp_size,) + blocks.shape)
+    spread = spread.reshape(grp_size * tok_size, count * share)
+    landed = lax.all_to_all(spread, ("grp", "tok"), 0, 0, tiled=True)
+    return jnp.sum(landed, axis=0).reshape(count, share)
 
 
 def layer_norm(value, gain, shift):
@@ -36,17 +108,6 @@
 def feature_map(logits):
     return jnp.concatenate(
         [jax.nn.softmax(logits, axis=-1), jax.nn.softmax(-logits, axis=-1)], axis=-1
-    )
-
-
-def chain_step(earlier, later):
-    flag_early, state_early, normer_early = earlier
-    flag_late, state_late, normer_late = later
-    retain = 1.0 - flag_late
-    return (
-        jnp.maximum(flag_early, flag_late),
-        state_late + retain * state_early,
-        normer_late + retain * normer_early,
     )
 
 
@@ -94,15 +155,16 @@
     tail_keys = jnp.where(closing[:, None, None], phi_key, jnp.zeros_like(phi_key))
     state_local = jnp.einsum("shf,shd->hfd", tail_keys, values, preferred_element_type=jnp.float32)
     normer_local = jnp.sum(tail_keys, axis=0, dtype=jnp.float32)
-    carried = entering(
-        (reset_flag, state_local, normer_local),
-        ("grp", "tok"),
-        chain_step,
-        (jnp.zeros((), jnp.float32), jnp.zeros_like(state_local), jnp.zeros_like(normer_local)),
-        False,
-    )
-    state_in = carried[1]
-    normer_in = carried[2]
+    def pack(state, normer):
+        return jnp.concatenate(
+            [state.transpose(0, 2, 1).reshape(model_width, 2 * head_dim), normer], axis=0
+        )
+
+    def unpack(packed):
+        state = packed[:model_width].reshape(head_count, head_dim, 2 * head_dim)
+        return state.transpose(0, 2, 1), packed[model_width:]
+
+    state_in, normer_in = unpack(carry_scan(pack(state_local, normer_local), 1.0 - reset_flag, False))
 
     def block_weights(offset):
         scores = jnp.einsum(
@@ -196,15 +258,9 @@
         open_query = query_wide * open_rows[:, None, None]
         grad_state = grad_state + jnp.einsum("thf,thd->hfd", open_query, dnumer, precision=highest)
         grad_normer = grad_normer + jnp.einsum("th,thf->hf", ddenom, open_query, precision=highest)
-    returned = entering(
-        (reset_flag, grad_state, grad_normer),
-        ("grp", "tok"),
-        chain_step,
-        (jnp.zeros((), jnp.float32), jnp.zeros_like(grad_state), jnp.zeros_like(grad_normer)),
-        True,
-    )
-    back_state = returned[1]
-    back_normer = returned[2]
+    back_state, back_normer = unpack(
+        carry_scan(pack(grad_state, grad_normer), 1.0 - reset_flag, True)
+    )
     closing_wide = closing.astype(jnp.float32)[:, None, None]
     grad_phik = grad_phik + closing_wide * (
         jnp.einsum("shd,hfd->shf", values.astype(jnp.float32), back_state, precision=highest)
@@ -238,32 +294,21 @@
     dhidden1 = jnp.dot(dpacked, w_qkv.T, preferred_element_type=jnp.float32)
     dx_norm, grad_g1, grad_b1 = ln1_back(dhidden1)
     grad_input = dresid + dx_norm
-    norm_stack = jnp.stack([grad_g1, grad_b1, grad_g2, grad_b2], axis=1)
-    shares = (
-        lax.psum_scatter(norm_stack, "tok", scatter_dimension=0, tiled=True),
-        lax.psum_scatter(grad_qkv, "tok", scatter_dimension=0, tiled=True),
-        lax.psum_scatter(grad_featq, "tok", scatter_dimension=0, tiled=True),
-        lax.psum_scatter(grad_featk, "tok", scatter_dimension=0, tiled=True),
-        lax.psum_scatter(grad_out, "tok", scatter_dimension=0, tiled=True),
-        lax.psum_scatter(grad_fc, "tok", scatter_dimension=0, tiled=True),
-        lax.psum_scatter(grad_proj, "tok", scatter_dimension=0, tiled=True),
-    )
-    shares = lax.psum(
-        (shares[0], shares[1], shares[2], shares[3], shares[4], shares[5], shares[6]), "grp"
-    )
+    vectors = reduce_vectors(jnp.stack([grad_g1, grad_b1, grad_g2, grad_b2]))
+    share_feat = reduce_rows(jnp.concatenate([grad_featq, grad_featk], axis=1))
     return (
         output,
         grad_input,
-        shares[0][:, 0],
-        shares[0][:, 1],
-        shares[1],
-        shares[2],
-        shares[3],
-        shares[4],
-        shares[0][:, 2],
-        shares[0][:, 3],
-        shares[5],
-        shares[6],
+        vectors[0],
+        vectors[1],
+        reduce_rows(grad_qkv),
+        share_feat[:, :head_dim],
+        share_feat[:, head_dim:],
+        reduce_rows(grad_out),
+        vectors[2],
+        vectors[3],
+        reduce_rows(grad_fc),
+        reduce_rows(grad_proj),
     )
 
 

time: 1490 us -> 716 us (0.48)
  waiting for transfers between devices: 428 us -> 171 us
  blocking collectives: 204 us -> 0 us
  local copies, waits for them, and re-layouts: 260 us -> 92.1 us
  other arithmetic: 244 us -> 123 us
  starting transfers between devices: 0.41 us -> 68.9 us
  loops' own time: 40.7 us -> 0 us
  matrix products: 277 us -> 248 us
    reduce_scatter x4 -> x0, waiting for transfers between devices: 198 us -> none  [the longest x1 132 us: on_device(): lax.psum_scatter(grad_qkv, 'tok', scatter_dimension=0, tiled=True)]
    select_n x124 -> x26, other arithmetic: 190 us -> 11.9 us  [the longest x8 5.4 us: carry_scan(): late = jnp.where(later, total, other)]
    ppermute x0 -> x45, waiting for transfers between devices: none -> 171 us  [the longest x20 108 us: reduce_rows(): lax.ppermute(give, axes, flips(grp_size, tok_size, flip_a, flip_b))]
    unnamed x13 -> x0, waiting for transfers between devices: 168 us -> none
    dynamic_slice x124 -> x20, local copies, waits for them, and re-layouts: 157 us -> 7.51 us  [reduce_rows(): give = lax.dynamic_slice_in_dim(buf, (1 - bit) * half, half, 0)]
    all_gather x2 -> x0, blocking collectives: 148 us -> none  [entering(): pieces = jax.tree.map(lambda part: lax.all_gather(part, axis), value)]
    ppermute x0 -> x45, starting transfers between devices: none -> 63.6 us  [the longest x10 30.9 us: reduce_rows(): other = lax.ppermute(buf, axes, flips(grp_size, tok_size, flip, flip))]
    psum x1 -> x0, waiting for transfers between devices: 61.5 us -> none  [on_device(): lax.psum((shares[0], shares[1], shares[2], shares[3], shares[4], shares[5...]
  transfers between devices with their start and end apart: 10 -> 46, of which waited for: 6 -> 21; matrix products, arithmetic and copies ran while one was open for 29% -> 34% of each run, Pallas kernels for 0% -> 0%
where the time goes in v1:
time: 716 us; the launch traced here: 707 us
  matrix products  248 us (35%)
  waiting for transfers between devices  171 us (24%)
  other arithmetic  123 us (17%)
  local copies, waits for them, and re-layouts  92.1 us (13%)
  starting transfers between devices  68.9 us (10%)
    ppermute x20, waiting for transfers between devices, reduce_rows(): lax.ppermute(give, axes, flips(grp_size, tok_size, flip_a, flip_b))  108 us
    ppermute x10, waiting for transfers between devices, carry_scan(): lax.ppermute(total, ('grp', 'tok'), flips(grp_size, tok_size, 1 << step,...  40.5 us
    unnamed x334, local copies, waits for them, and re-layouts  35.3 us
    ppermute x10, starting transfers between devices, reduce_rows(): other = lax.ppermute(buf, axes, flips(grp_size, tok_size, flip, flip))  30.9 us
    dot_general x2, matrix products, on_device(): jnp.einsum('hts,shf->thf', dweights, phi_key, preferred_element_type=jnp....  23.2 us
    ppermute x10, waiting for transfers between devices, reduce_rows(): other = lax.ppermute(buf, axes, flips(grp_size, tok_size, flip, flip))  22.7 us
    add x8, other arithmetic, carry_scan(): total = jnp.where(is_keep, 0.0, late) + late[rows, 0] * early  21.8 us
    ppermute x20, starting transfers between devices, reduce_rows(): lax.ppermute(give, axes, flips(grp_size, tok_size, flip_a, flip_b))  20 us
  transfers between devices with their start and end apart: 46, of which 21 were waited for; matrix products, arithmetic and copies ran while one was open for 34% of the time, Pallas kernels for 0%

profile of v1, /device:TPU:0, one launch (start us, length us, event | category | flops | bytes accessed | tf_op | source)
XLA Modules:
  0.0 707.1 jit_solution(6483171507817495283)
XLA Ops:
  70.7 7.9 %convert_reduce_fusion = (f32[12,512]{1,0:T(8,128)}, bf16[12,512,1024]{2,1,0:T(8,128)(2,1)}) fusion(bf16[512,12,128]{0,2,1:T(8,128)(2,1)S(1)} %get-tuple-element.80, bf16[1024,12,64]{0,2,1:T(8,128)(2,1)S(1)} %copy-done.12, bf16[1024,12,64]{0,2,1:T(8,128)(2,1)S(1)} %copy-done.15, pred[512,1024]{1,0:T(8,128)(4,1)S(1)} %get-tuple-element.124), kind=kOutput, calls=%fused_computation.6 | convolution fusion | flops 1642063872 | bytes 17850368 | tf_op jit(solution)/shard_map/thf,shf->hts/dot_general | solution.py:170
  85.8 10.2 %convert_reduce_fusion.1 = (f32[12,512]{1,0:T(8,128)}, bf16[12,512,1024]{2,1,0:T(8,128)(2,1)}) fusion(bf16[512,12,128]{0,2,1:T(8,128)(2,1)} %get-tuple-element.79, bf16[1024,12,64]{0,2,1:T(8,128)(2,1)} %copy-done.11, bf16[1024,12,64]{0,2,1:T(8,128)(2,1)} %copy-done.14, pred[512,1024]{1,0:T(8,128)(4,1)} %get-tuple-element.123), kind=kOutput, calls=%fused_computation.8 | convolution fusion | flops 1642063872 | bytes 17850368 | tf_op jit(solution)/shard_map/thf,shf->hts/dot_general | solution.py:170
  105.0 9.7 %fusion.119 = f32[12,64,512]{2,1,0:T(8,128)} fusion(bf16[1024,12,64]{0,2,1:T(8,128)(2,1)S(1)} %bitcast.311, bf16[12,512,1024]{2,1,0:T(8,128)(2,1)} %get-tuple-element.140), kind=kOutput, calls=%fused_computation.320 | convolution fusion | flops 805306368 | bytes 15728640 | tf_op jit(solution)/shard_map/hts,shd->thd/dot_general | solution.py:187
  116.0 6.6 collective-permute-done.2
  127.8 9.6 %fusion.118 = f32[12,64,512]{2,1,0:T(8,128)} fusion(bf16[1024,12,64]{0,2,1:T(8,128)(2,1)S(1)} %bitcast.312, bf16[12,512,1024]{2,1,0:T(8,128)(2,1)} %get-tuple-element.144), kind=kOutput, calls=%fused_computation.319 | convolution fusion | flops 805306368 | bytes 15728640 | tf_op jit(solution)/shard_map/hts,shd->thd/dot_general | solution.py:187
  150.2 9.0 %collective-permute-done.4 = f32[784,128]{1,0:T(8,128)S(1)} collective-permute-done((f32[784,128]{1,0:T(8,128)S(1)}, f32[784,128]{1,0:T(8,128)S(1)}, u32[]{:S(2)}, u32[]{:S(2)}) %collective-permute-start.4) | collective-permute-done | bytes 401440 | tf_op jit(solution)/shard_map/ppermute | solution.py:33
  171.4 8.6 %fusion.97 = f32[1024,3072]{1,0:T(8,128)} fusion(bf16[768,3072]{1,0:T(8,128)(2,1)S(1)} %bitcast.341, f32[1024,768]{0,1:T(8,128)S(1)} %get-tuple-element.148, f32[768]{0:T(1024)S(1)} %copy-done.90, f32[768]{0:T(1024)S(1)} %copy-done.89, f32[1024]{0:T(1024)S(1)} %fusion.86, f32[1024]{0:T(1024)S(1)} %broadcast_multiply_fusion), kind=kOutput, calls=%fused_computation.298 | convolution fusion | flops 4835770368 | bytes 20461568 | tf_op jit(solution)/shard_map/dot_general | solution.py:204
  180.0 10.1 %add_convert_fusion.3 = bf16[1024,768]{0,1:T(8,128)(2,1)} fusion(f32[1024,768]{0,1:T(8,128)S(1)} %get-tuple-element.148, bf16[3072,768]{1,0:T(8,128)(2,1)S(1)} %bitcast.385, f32[1024,3072]{1,0:T(8,128)} %fusion.97), kind=kOutput, calls=%fused_computation.89 | convolution fusion | flops 4861722624 | bytes 22020096 | tf_op jit(solution)/shard_map/dot_general | solution.py:207
  190.1 15.8 %fusion.10 = bf16[1024,3072]{1,0:T(8,128)(2,1)} fusion(f32[1024,3072]{1,0:T(8,128)} %fusion.97, bf16[1024,768]{1,0:T(8,128)(2,1)S(1)} %copy-done.58, bf16[3072,768]{1,0:T(8,128)(2,1)S(1)} %bitcast.385), kind=kOutput, calls=%fused_computation.18 | convolution fusion | flops 4894752768 | bytes 25165824 | tf_op jit(solution)/shard_map/dot_general | solution.py:211
  205.9 12.5 %fusion.100 = f32[3072,768]{1,0:T(8,128)} fusion(bf16[1024,768]{1,0:T(8,128)(2,1)S(1)} %copy-done.58, f32[1024,3072]{1,0:T(8,128)} %fusion.97), kind=kOutput, calls=%fused_computation.301 | convolution fusion | flops 4860149760 | bytes 23592960 | tf_op jit(solution)/shard_map/dot_general | solution.py:210
  218.4 7.3 %fusion.116 = (f32[768]{0:T(1024)}, f32[1024,768]{1,0:T(8,128)}) fusion(bf16[1024,3072]{1,0:T(8,128)(2,1)S(1)} %copy-done.137, bf16[768,3072]{1,0:T(8,128)(2,1)S(1)} %bitcast.341), kind=kOutput, calls=%fused_computation.317 | convolution fusion | flops 4832623616 | bytes 14158848 | tf_op jit(solution)/shard_map/dot_general | solution.py:214
  225.7 7.8 %fusion.96 = f32[768,3072]{1,0:T(8,128)} fusion(bf16[1024,3072]{1,0:T(8,128)(2,1)S(1)} %copy-done.137, f32[1024,768]{0,1:T(8,128)S(1)} %get-tuple-element.148, f32[768]{0:T(1024)S(1)} %copy-done.90, f32[768]{0:T(1024)S(1)} %copy-done.89, f32[1024]{0:T(1024)S(1)} %fusion.86, f32[1024]{0:T(1024)S(1)} %broadcast_multiply_fusion), kind=kOutput, calls=%fused_computation.297 | convolution fusion | flops 4835770368 | bytes 18888704 | tf_op jit(solution)/shard_map/dot_general | solution.py:213
  266.3 7.7 %select_convert_fusion.1 = bf16[12,512,1024]{2,1,0:T(8,128)(2,1)} fusion(f32[12,512]{1,0:T(8,128)S(1)} %bitcast_divide_fusion.3, pred[512,1024]{1,0:T(8,128)(4,1)S(1)} %copy-done.88, bf16[1024,12,64]{0,2,1:T(8,128)(2,1)S(1)} %bitcast.313, f32[512,12,64]{0,2,1:T(8,128)S(1)} %bitcast.301, f32[512,12]{0,1:T(8,128)S(1)} %copy-done.84), kind=kOutput, calls=%fused_computation.5 | convolution fusion | flops 824967168 | bytes 16302080 | tf_op jit(solution)/shard_map/thd,shd->hts/dot_general | solution.py:240
  274.1 11.5 %fusion.99 = f32[12,128,512]{2,1,0:T(8,128)} fusion(bf16[12,512,1024]{2,1,0:T(8,128)(2,1)} %select_convert_fusion.1, bf16[1024,12,64]{0,2,1:T(8,128)(2,1)} %copy-done.11, bf16[1024,12,64]{0,2,1:T(8,128)(2,1)} %copy-done.14), kind=kOutput, calls=%fused_computation.300 | convolution fusion | flops 1616904192 | bytes 18874368 | tf_op jit(solution)/shard_map/hts,shf->thf/dot_general | solution.py:244
  285.6 9.6 %fusion.120 = f32[12,128,1024]{2,1,0:T(8,128)} fusion(bf16[512,12,128]{0,2,1:T(8,128)(2,1)} %get-tuple-element.79, bf16[12,512,1024]{2,1,0:T(8,128)(2,1)} %select_convert_fusion.1), kind=kOutput, calls=%fused_computation.321 | convolution fusion | flops 1610612736 | bytes 20447232 | tf_op jit(solution)/shard_map/hts,thf->shf/dot_general | solution.py:252
  305.6 7.5 %select_convert_fusion = bf16[12,512,1024]{2,1,0:T(8,128)(2,1)} fusion(f32[12,512]{1,0:T(8,128)S(1)} %copy-done.122, pred[512,1024]{1,0:T(8,128)(4,1)S(1)} %copy-done.87, bf16[1024,12,64]{0,2,1:T(8,128)(2,1)S(1)} %bitcast.314, f32[512,12,64]{0,2,1:T(8,128)S(1)} %bitcast.297, f32[512,12]{0,1:T(8,128)S(1)} %copy-done.81), kind=kOutput, calls=%fused_computation.4 | convolution fusion | flops 824967168 | bytes 16302080 | tf_op jit(solution)/shard_map/thd,shd->hts/dot_general | solution.py:240
  313.2 11.6 %fusion.98 = f32[12,128,512]{2,1,0:T(8,128)} fusion(bf16[12,512,1024]{2,1,0:T(8,128)(2,1)} %select_convert_fusion, bf16[1024,12,64]{0,2,1:T(8,128)(2,1)} %copy-done.11, bf16[1024,12,64]{0,2,1:T(8,128)(2,1)} %copy-done.14), kind=kOutput, calls=%fused_computation.299 | convolution fusion | flops 1616904192 | bytes 18874368 | tf_op jit(solution)/shard_map/hts,shf->thf/dot_general | solution.py:244
  324.8 5.7 fusion.26
  348.7 7.1 %collective-permute-done.6 = f32[784,128]{1,0:T(8,128)S(1)} collective-permute-done((f32[784,128]{1,0:T(8,128)S(1)}, f32[784,128]{1,0:T(8,128)S(1)}, u32[]{:S(2)}, u32[]{:S(2)}) %collective-permute-start.6) | collective-permute-done | bytes 401440 | tf_op jit(solution)/shard_map/ppermute | solution.py:33
  362.1 16.4 %collective-permute-done.7 = f32[784,128]{1,0:T(8,128)S(1)} collective-permute-done((f32[784,128]{1,0:T(8,128)S(1)}, f32[784,128]{1,0:T(8,128)S(1)}, u32[]{:S(2)}, u32[]{:S(2)}) %collective-permute-start.7) | collective-permute-done | bytes 401440 | tf_op jit(solution)/shard_map/ppermute | solution.py:33
  409.2 9.1 %add_bitcast_fusion = f32[1024,12,128]{0,2,1:T(8,128)S(1)} fusion(f32[12,128,1024]{2,1,0:T(8,128)} %fusion.121, f32[12,128,1024]{2,1,0:T(8,128)S(1)} %bitcast.287, f32[12,128]{1,0:T(8,128)S(1)} %slice-done.23, f32[1024]{0:T(1024)S(1)} %copy-done.109, bf16[512,12,128]{0,2,1:T(8,128)(2,1)S(1)} %copy-done.36, bf16[12,512,1024]{2,1,0:T(8,128)(2,1)} %select_convert_fusion), kind=kOutput, calls=%fused_computation.22 | convolution fusion | flops 1616904192 | bytes 33040384 | tf_op jit(solution)/shard_map/hts,thf->shf/dot_general | solution.py:252
  434.1 5.6 fusion.117
  452.4 6.8 add_add_fusion.2
  470.2 6.9 fusion.45
  541.7 5.5 collective-permute-done.39
  550.2 15.9 %collective-permute-done.11 = f32[8,24,2304]{2,1,0:T(8,128)} collective-permute-done((f32[8,24,2304]{2,1,0:T(8,128)}, f32[8,24,2304]{2,1,0:T(8,128)}, u32[]{:S(2)}, u32[]{:S(2)}) %collective-permute-start.11) | collective-permute-done | bytes 1769504 | tf_op jit(solution)/shard_map/ppermute | solution.py:79
  568.0 23.4 %collective-permute-done.32 = f32[8,24,3072]{2,1,0:T(8,128)} collective-permute-done((f32[8,24,3072]{2,1,0:T(8,128)}, f32[8,24,3072]{2,1,0:T(8,128)}, u32[]{:S(2)}, u32[]{:S(2)}) %collective-permute-start.32) | collective-permute-done | bytes 2359328 | tf_op jit(solution)/shard_map/ppermute | solution.py:79
  600.5 22.8 %collective-permute-done.33 = f32[4,24,3072]{2,1,0:T(8,128)S(1)} collective-permute-done((f32[4,24,3072]{2,1,0:T(8,128)S(1)}, f32[4,24,3072]{2,1,0:T(8,128)S(1)}, u32[]{:S(2)}, u32[]{:S(2)}) %collective-permute-start.33) | collective-permute-done | bytes 1179680 | tf_op jit(solution)/shard_map/ppermute | solution.py:79
  626.9 28.3 %collective-permute-done.34 = f32[2,24,3072]{2,1,0:T(8,128)S(1)} collective-permute-done((f32[2,24,3072]{2,1,0:T(8,128)S(1)}, f32[2,24,3072]{2,1,0:T(8,128)S(1)}, u32[]{:S(2)}, u32[]{:S(2)}) %collective-permute-start.34) | collective-permute-done | bytes 589856 | tf_op jit(solution)/shard_map/ppermute | solution.py:79
  661.4 25.8 %collective-permute-start.16 = (f32[2,24,2304]{2,1,0:T(8,128)S(1)}, f32[2,24,2304]{2,1,0:T(8,128)S(1)}, u32[]{:S(2)}, u32[]{:S(2)}) collective-permute-start(f32[2,24,2304]{2,1,0:T(8,128)S(1)} %pad_maximum_fusion.12), channel_id=1, source_target_pairs={{0,8},{1,9},{2,10},{3,11},{4,12},{5,13},{6,14},{7,15},{8,0},{9,1},... | collective-permute-start | bytes 1327112 | tf_op jit(solution)/shard_map/ppermute | solution.py:82
  689.4 7.7 %collective-permute-done.43 = f32[1,96,768]{2,1,0:T(8,128)S(1)} collective-permute-done((f32[1,96,768]{2,1,0:T(8,128)S(1)}, f32[1,96,768]{2,1,0:T(8,128)S(1)}, u32[]{:S(2)}, u32[]{:S(2)}) %collective-permute-start.43) | collective-permute-done | bytes 294944 | tf_op jit(solution)/shard_map/ppermute | solution.py:82
  697.3 5.7 collective-permute-done.36
  (651 shorter events, 347.5 us)
Async XLA Ops:
  45.4 33.7 %collective-permute-start = (f32[784,128]{1,0:T(8,128)}, f32[784,128]{1,0:T(8,128)}, u32[]{:S(2)}, u32[]{:S(2)}) collective-permute-start(f32[784,128]{1,0:T(8,128)} %maximum_maximum_fusion), channel_id=1, source_target_pairs={{0,1},{1,0},{2,3},{3,2},{4,5},{5,4},{6,7},{7,6},{8,9},{9,8},{10,11... | collective-permute-start | bytes 1204232 | tf_op jit(solution)/shard_map/ppermute | solution.py:33
  84.2 13.0 %collective-permute-start.1 = (f32[784,128]{1,0:T(8,128)}, f32[784,128]{1,0:T(8,128)}, u32[]{:S(2)}, u32[]{:S(2)}) collective-permute-start(f32[784,128]{1,0:T(8,128)} %get-tuple-element.107), channel_id=1, source_target_pairs={{0,2},{1,3},{2,0},{3,1},{4,6},{5,7},{6,4},{7,5},{8,10},{9,11},{10,... | collective-permute-start | bytes 1204232 | tf_op jit(solution)/shard_map/ppermute | solution.py:33
  102.4 20.2 %collective-permute-start.2 = (f32[784,128]{1,0:T(8,128)}, f32[784,128]{1,0:T(8,128)}, u32[]{:S(2)}, u32[]{:S(2)}) collective-permute-start(f32[784,128]{1,0:T(8,128)} %get-tuple-element.105), channel_id=1, source_target_pairs={{0,4},{1,5},{2,6},{3,7},{4,0},{5,1},{6,2},{7,3},{8,12},{9,13},{10,... | collective-permute-start | bytes 1204232 | tf_op jit(solution)/shard_map/ppermute | solution.py:33
  127.8 15.3 %collective-permute-start.3 = (f32[784,128]{1,0:T(8,128)}, f32[784,128]{1,0:T(8,128)}, u32[]{:S(2)}, u32[]{:S(2)}) collective-permute-start(f32[784,128]{1,0:T(8,128)} %get-tuple-element.103), channel_id=1, source_target_pairs={{0,8},{1,9},{2,10},{3,11},{4,12},{5,13},{6,14},{7,15},{8,0},{9,1},... | collective-permute-start | bytes 1204232 | tf_op jit(solution)/shard_map/ppermute | solution.py:33
  147.4 11.8 %collective-permute-start.4 = (f32[784,128]{1,0:T(8,128)S(1)}, f32[784,128]{1,0:T(8,128)S(1)}, u32[]{:S(2)}, u32[]{:S(2)}) collective-permute-start(f32[784,128]{1,0:T(8,128)S(1)} %get-tuple-element.101), channel_id=1, source_target_pairs={{0,16},{1,17},{2,18},{3,19},{4,20},{5,21},{6,22},{7,23},{8,24},{9,... | collective-permute-start | bytes 1204232 | tf_op jit(solution)/shard_map/ppermute | solution.py:33
  305.2 34.6 %collective-permute-start.5 = (f32[784,128]{1,0:T(8,128)}, f32[784,128]{1,0:T(8,128)}, u32[]{:S(2)}, u32[]{:S(2)}) collective-permute-start(f32[784,128]{1,0:T(8,128)} %maximum_maximum_fusion.1), channel_id=1, source_target_pairs={{0,1},{1,0},{2,3},{3,2},{4,5},{5,4},{6,7},{7,6},{8,9},{9,8},{10,11... | collective-permute-start | bytes 1204232 | tf_op jit(solution)/shard_map/ppermute | solution.py:33
  339.7 22.3 %collective-permute-start.24 = (f32[8,48,768]{2,1,0:T(8,128)S(1)}, f32[8,48,768]{2,1,0:T(8,128)S(1)}, u32[]{:S(2)}, u32[]{:S(2)}) collective-permute-start(f32[8,48,768]{2,1,0:T(8,128)S(1)} %dynamic-slice_bitcast_fusion.3), channel_id=1, source_target_pairs={{0,8},{1,9},{2,10},{3,11},{4,12},{5,13},{6,14},{7,15},{8,0},{9,1},... | collective-permute-start | bytes 3538952 | tf_op jit(solution)/shard_map/ppermute | solution.py:57
  358.2 20.4 %collective-permute-start.7 = (f32[784,128]{1,0:T(8,128)S(1)}, f32[784,128]{1,0:T(8,128)S(1)}, u32[]{:S(2)}, u32[]{:S(2)}) collective-permute-start(f32[784,128]{1,0:T(8,128)S(1)} %get-tuple-element.97), channel_id=1, source_target_pairs={{0,4},{1,5},{2,6},{3,7},{4,0},{5,1},{6,2},{7,3},{8,12},{9,13},{10,... | collective-permute-start | bytes 1204232 | tf_op jit(solution)/shard_map/ppermute | solution.py:33
  382.8 13.6 %collective-permute-start.25 = (f32[8,24,768]{2,1,0:T(8,128)}, f32[8,24,768]{2,1,0:T(8,128)}, u32[]{:S(2)}, u32[]{:S(2)}) collective-permute-start(f32[8,24,768]{2,1,0:T(8,128)} %constant_dynamic-slice_fusion.11), channel_id=1, source_target_pairs={{0,16},{1,17},{2,18},{3,19},{4,20},{5,21},{6,22},{7,23},{8,9},{9,8... | collective-permute-start | bytes 1769480 | tf_op jit(solution)/shard_map/ppermute | solution.py:79
  387.8 13.8 %collective-permute-start.9 = (f32[784,128]{1,0:T(8,128)}, f32[784,128]{1,0:T(8,128)}, u32[]{:S(2)}, u32[]{:S(2)}) collective-permute-start(f32[784,128]{1,0:T(8,128)} %get-tuple-element.93), channel_id=1, source_target_pairs={{0,16},{1,17},{2,18},{3,19},{4,20},{5,21},{6,22},{7,23},{8,24},{9,... | collective-permute-start | bytes 1204232 | tf_op jit(solution)/shard_map/ppermute | solution.py:33
  394.2 116.8 %collective-permute-start.38 = (f32[8,192,768]{2,1,0:T(8,128)}, f32[8,192,768]{2,1,0:T(8,128)}, u32[]{:S(2)}, u32[]{:S(2)}) collective-permute-start(f32[8,192,768]{2,1,0:T(8,128)} %dynamic-slice_bitcast_fusion), channel_id=1, source_target_pairs={{0,8},{1,9},{2,10},{3,11},{4,12},{5,13},{6,14},{7,15},{8,0},{9,1},... | collective-permute-start | bytes 14155784 | tf_op jit(solution)/shard_map/ppermute | solution.py:57
  395.2 124.7 %collective-permute-start.31 = (f32[8,48,3072]{2,1,0:T(8,128)}, f32[8,48,3072]{2,1,0:T(8,128)}, u32[]{:S(2)}, u32[]{:S(2)}) collective-permute-start(f32[8,48,3072]{2,1,0:T(8,128)} %dynamic-slice_bitcast_fusion.1), channel_id=1, source_target_pairs={{0,8},{1,9},{2,10},{3,11},{4,12},{5,13},{6,14},{7,15},{8,0},{9,1},... | collective-permute-start | bytes 14155784 | tf_op jit(solution)/shard_map/ppermute | solution.py:57
  398.6 82.7 %collective-permute-start.26 = (f32[4,24,768]{2,1,0:T(8,128)}, f32[4,24,768]{2,1,0:T(8,128)}, u32[]{:S(2)}, u32[]{:S(2)}) collective-permute-start(f32[4,24,768]{2,1,0:T(8,128)} %constant_dynamic-slice_fusion.10), channel_id=1, source_target_pairs={{0,1},{1,0},{2,3},{3,2},{4,5},{5,4},{6,7},{7,6},{8,10},{9,11},{10,... | collective-permute-start | bytes 884744 | tf_op jit(solution)/shard_map/ppermute | solution.py:79
  431.9 54.9 %collective-permute-start.17 = (f32[8,48,128]{2,1,0:T(8,128)}, f32[8,48,128]{2,1,0:T(8,128)}, u32[]{:S(2)}, u32[]{:S(2)}) collective-permute-start(f32[8,48,128]{2,1,0:T(8,128)} %fusion.74), channel_id=1, source_target_pairs={{0,8},{1,9},{2,10},{3,11},{4,12},{5,13},{6,14},{7,15},{8,0},{9,1},... | collective-permute-start | bytes 589832 | tf_op jit(solution)/shard_map/ppermute | solution.py:57
  464.8 20.5 %all-to-all-start = ((f32[32,1,384]{2,1,0:T(1,128)}), f32[32,1,384]{2,1,0:T(1,128)}, u32[]{:S(2)}, u32[]{:S(2)}) async-start(f32[32,1,384]{2,1,0:T(1,128)} %all_to_all.6), calls=%async_computation | async-start | bytes 98304 | tf_op jit(solution)/shard_map/all_to_all | solution.py:97
  481.1 45.2 %collective-permute-start.10 = (f32[8,48,2304]{2,1,0:T(8,128)}, f32[8,48,2304]{2,1,0:T(8,128)}, u32[]{:S(2)}, u32[]{:S(2)}) collective-permute-start(f32[8,48,2304]{2,1,0:T(8,128)} %dynamic-slice_bitcast_fusion.2), channel_id=1, source_target_pairs={{0,8},{1,9},{2,10},{3,11},{4,12},{5,13},{6,14},{7,15},{8,0},{9,1},... | collective-permute-start | bytes 10616840 | tf_op jit(solution)/shard_map/ppermute | solution.py:57
  508.4 31.5 %collective-permute-start.30 = (f32[2,24,768]{2,1,0:T(8,128)}, f32[2,24,768]{2,1,0:T(8,128)}, u32[]{:S(2)}, u32[]{:S(2)}) collective-permute-start(f32[2,24,768]{2,1,0:T(8,128)} %pad_maximum_fusion.14), channel_id=1, source_target_pairs={{0,8},{1,9},{2,10},{3,11},{4,12},{5,13},{6,14},{7,15},{8,0},{9,1},... | collective-permute-start | bytes 442376 | tf_op jit(solution)/shard_map/ppermute | solution.py:82
  510.9 25.3 %collective-permute-start.23 = (f32[2,24,128]{2,1,0:T(8,128)S(1)}, f32[2,24,128]{2,1,0:T(8,128)S(1)}, u32[]{:S(2)}, u32[]{:S(2)}) collective-permute-start(f32[2,24,128]{2,1,0:T(8,128)S(1)} %pad_maximum_fusion.16), channel_id=1, source_target_pairs={{0,8},{1,9},{2,10},{3,11},{4,12},{5,13},{6,14},{7,15},{8,0},{9,1},... | collective-permute-start | bytes 73736 | tf_op jit(solution)/shard_map/ppermute | solution.py:82
  518.0 29.2 %collective-permute-start.39 = (f32[8,96,768]{2,1,0:T(8,128)}, f32[8,96,768]{2,1,0:T(8,128)}, u32[]{:S(2)}, u32[]{:S(2)}) collective-permute-start(f32[8,96,768]{2,1,0:T(8,128)} %constant_dynamic-slice_fusion.3), channel_id=1, source_target_pairs={{0,16},{1,17},{2,18},{3,19},{4,20},{5,21},{6,22},{7,23},{8,9},{9,8... | collective-permute-start | bytes 7077896 | tf_op jit(solution)/shard_map/ppermute | solution.py:79
  532.5 33.6 %collective-permute-start.11 = (f32[8,24,2304]{2,1,0:T(8,128)}, f32[8,24,2304]{2,1,0:T(8,128)}, u32[]{:S(2)}, u32[]{:S(2)}) collective-permute-start(f32[8,24,2304]{2,1,0:T(8,128)} %constant_dynamic-slice_fusion.20), channel_id=1, source_target_pairs={{0,16},{1,17},{2,18},{3,19},{4,20},{5,21},{6,22},{7,23},{8,9},{9,8... | collective-permute-start | bytes 5308424 | tf_op jit(solution)/shard_map/ppermute | solution.py:79
  534.8 56.7 %collective-permute-start.32 = (f32[8,24,3072]{2,1,0:T(8,128)}, f32[8,24,3072]{2,1,0:T(8,128)}, u32[]{:S(2)}, u32[]{:S(2)}) collective-permute-start(f32[8,24,3072]{2,1,0:T(8,128)} %constant_dynamic-slice_fusion.7), channel_id=1, source_target_pairs={{0,16},{1,17},{2,18},{3,19},{4,20},{5,21},{6,22},{7,23},{8,9},{9,8... | collective-permute-start | bytes 7077896 | tf_op jit(solution)/shard_map/ppermute | solution.py:79
  550.1 48.1 %collective-permute-start.40 = (f32[4,96,768]{2,1,0:T(8,128)S(1)}, f32[4,96,768]{2,1,0:T(8,128)S(1)}, u32[]{:S(2)}, u32[]{:S(2)}) collective-permute-start(f32[4,96,768]{2,1,0:T(8,128)S(1)} %constant_dynamic-slice_fusion.2), channel_id=1, source_target_pairs={{0,1},{1,0},{2,3},{3,2},{4,5},{5,4},{6,7},{7,6},{8,10},{9,11},{10,... | collective-permute-start | bytes 3538952 | tf_op jit(solution)/shard_map/ppermute | solution.py:79
  567.9 30.1 %collective-permute-start.12 = (f32[4,24,2304]{2,1,0:T(8,128)S(1)}, f32[4,24,2304]{2,1,0:T(8,128)S(1)}, u32[]{:S(2)}, u32[]{:S(2)}) collective-permute-start(f32[4,24,2304]{2,1,0:T(8,128)S(1)} %constant_dynamic-slice_fusion.19), channel_id=1, source_target_pairs={{0,1},{1,0},{2,3},{3,2},{4,5},{5,4},{6,7},{7,6},{8,10},{9,11},{10,... | collective-permute-start | bytes 2654216 | tf_op jit(solution)/shard_map/ppermute | solution.py:79
  593.5 29.8 %collective-permute-start.33 = (f32[4,24,3072]{2,1,0:T(8,128)S(1)}, f32[4,24,3072]{2,1,0:T(8,128)S(1)}, u32[]{:S(2)}, u32[]{:S(2)}) collective-permute-start(f32[4,24,3072]{2,1,0:T(8,128)S(1)} %constant_dynamic-slice_fusion.6), channel_id=1, source_target_pairs={{0,1},{1,0},{2,3},{3,2},{4,5},{5,4},{6,7},{7,6},{8,10},{9,11},{10,... | collective-permute-start | bytes 3538952 | tf_op jit(solution)/shard_map/ppermute | solution.py:79
  598.2 25.4 %collective-permute-start.13 = (f32[2,24,2304]{2,1,0:T(8,128)S(1)}, f32[2,24,2304]{2,1,0:T(8,128)S(1)}, u32[]{:S(2)}, u32[]{:S(2)}) collective-permute-start(f32[2,24,2304]{2,1,0:T(8,128)S(1)} %constant_dynamic-slice_fusion.18), channel_id=1, source_target_pairs={{0,2},{1,3},{2,0},{3,1},{4,6},{5,7},{6,4},{7,5},{8,12},{9,13},{10,... | collective-permute-start | bytes 1327112 | tf_op jit(solution)/shard_map/ppermute | solution.py:79
  598.4 28.2 %collective-permute-start.41 = (f32[2,96,768]{2,1,0:T(8,128)S(1)}, f32[2,96,768]{2,1,0:T(8,128)S(1)}, u32[]{:S(2)}, u32[]{:S(2)}) collective-permute-start(f32[2,96,768]{2,1,0:T(8,128)S(1)} %constant_dynamic-slice_fusion.1), channel_id=1, source_target_pairs={{0,2},{1,3},{2,0},{3,1},{4,6},{5,7},{6,4},{7,5},{8,12},{9,13},{10,... | collective-permute-start | bytes 1769480 | tf_op jit(solution)/shard_map/ppermute | solution.py:79
  623.5 31.7 %collective-permute-start.34 = (f32[2,24,3072]{2,1,0:T(8,128)S(1)}, f32[2,24,3072]{2,1,0:T(8,128)S(1)}, u32[]{:S(2)}, u32[]{:S(2)}) collective-permute-start(f32[2,24,3072]{2,1,0:T(8,128)S(1)} %constant_dynamic-slice_fusion.5), channel_id=1, source_target_pairs={{0,2},{1,3},{2,0},{3,1},{4,6},{5,7},{6,4},{7,5},{8,12},{9,13},{10,... | collective-permute-start | bytes 1769480 | tf_op jit(solution)/shard_map/ppermute | solution.py:79
  623.7 31.5 %collective-permute-start.14 = (f32[1,24,2304]{2,1,0:T(8,128)S(1)}, f32[1,24,2304]{2,1,0:T(8,128)S(1)}, u32[]{:S(2)}, u32[]{:S(2)}) collective-permute-start(f32[1,24,2304]{2,1,0:T(8,128)S(1)} %constant_dynamic-slice_fusion.17), channel_id=1, source_target_pairs={{0,4},{1,5},{2,6},{3,7},{4,0},{5,1},{6,2},{7,3},{8,24},{9,25},{10,... | collective-permute-start | bytes 663560 | tf_op jit(solution)/shard_map/ppermute | solution.py:79
  626.8 60.4 %collective-permute-start.42 = (f32[1,96,768]{2,1,0:T(8,128)S(1)}, f32[1,96,768]{2,1,0:T(8,128)S(1)}, u32[]{:S(2)}, u32[]{:S(2)}) collective-permute-start(f32[1,96,768]{2,1,0:T(8,128)S(1)} %constant_dynamic-slice_fusion), channel_id=1, source_target_pairs={{0,4},{1,5},{2,6},{3,7},{4,0},{5,1},{6,2},{7,3},{8,24},{9,25},{10,... | collective-permute-start | bytes 884744 | tf_op jit(solution)/shard_map/ppermute | solution.py:79
  656.0 32.5 %collective-permute-start.35 = (f32[1,24,3072]{2,1,0:T(8,128)S(1)}, f32[1,24,3072]{2,1,0:T(8,128)S(1)}, u32[]{:S(2)}, u32[]{:S(2)}) collective-permute-start(f32[1,24,3072]{2,1,0:T(8,128)S(1)} %constant_dynamic-slice_fusion.4), channel_id=1, source_target_pairs={{0,4},{1,5},{2,6},{3,7},{4,0},{5,1},{6,2},{7,3},{8,24},{9,25},{10,... | collective-permute-start | bytes 884744 | tf_op jit(solution)/shard_map/ppermute | solution.py:79
  661.4 41.8 %collective-permute-start.16 = (f32[2,24,2304]{2,1,0:T(8,128)S(1)}, f32[2,24,2304]{2,1,0:T(8,128)S(1)}, u32[]{:S(2)}, u32[]{:S(2)}) collective-permute-start(f32[2,24,2304]{2,1,0:T(8,128)S(1)} %pad_maximum_fusion.12), channel_id=1, source_target_pairs={{0,8},{1,9},{2,10},{3,11},{4,12},{5,13},{6,14},{7,15},{8,0},{9,1},... | collective-permute-start | bytes 1327112 | tf_op jit(solution)/shard_map/ppermute | solution.py:82
  688.5 14.5 %collective-permute-start.36 = (f32[1,24,3072]{2,1,0:T(8,128)S(1)}, f32[1,24,3072]{2,1,0:T(8,128)S(1)}, u32[]{:S(2)}, u32[]{:S(2)}) collective-permute-start(f32[1,24,3072]{2,1,0:T(8,128)S(1)} %dynamic-slice_add_fusion.11), channel_id=1, source_target_pairs={{0,16},{1,17},{2,18},{3,19},{4,20},{5,21},{6,22},{7,23},{8,24},{9,... | collective-permute-start | bytes 884744 | tf_op jit(solution)/shard_map/ppermute | solution.py:82
  (180 other events, 1210.5 us)
